TPU v7x, 32 devices: a whole 2x2x4 slice. The times are simulated.
32 devices in a mesh: grp: 2 (over x), lon: 16 (over z, y, core).
Axes of the slice: x: 2, y: 2, z: 4, core: 2. Of those that a mesh axis runs over, the one named last changes fastest.
Arguments:
- tracer_pert: float32 [4, 50, 32, 1024], P('grp', None, 'lon'), parts along dimension 0, may hold values from -60 to 60
- surface_pert: float32 [4, 32, 1024], P('grp', 'lon'), parts along dimension 0, may hold values from -60 to 60
- zonal_flow: float32 [50, 32, 1024], P(None, 'lon'), may hold values from -3.2 to 3.2
- merid_flow: float32 [50, 32, 1024], P(None, 'lon'), may hold values from -3.2 to 3.2
- bottom_level: int32 [32, 1024], P('lon'), may hold values from 0 to 50
Outputs:
- tracer_vec: float32 [4, 50, 32, 1024], P('grp', None, 'lon'), parts along dimension 0
- surface_vec: float32 [4, 32, 1024], P('grp', 'lon'), parts along dimension 0
- growth: float32 [6], P('grp'), parts along dimension 0
There are 2 independent parts, one for each index of `grp`. A program takes and returns all parts, laid end to end along the dimension named above; an argument that names none is the same for every part. Nothing has to cross between parts.
Inputs may be any that keep to these rules, and one draw needn't show every extreme that they name: `bottom_level`: 0 marks a land column, 50 a column wet to the bottom level.
All inputs are finite; a program needn't handle non-finite values.
Results may differ from a plain program's by a relative error of at most 0.0001.
Values sent between devices are 32-bit elements; how exact they have to be, the bound alone decides.
A program may use at most 64 MiB of HBM per device.

v0:
```python
import jax
import jax.numpy as jnp
from jax import lax
from jax.sharding import PartitionSpec as P

ITERS = 3


DIFFUSIVITY = 0.5
TIME_STEP = 0.2
SURFACE_COUPLING = 0.5
STERIC_GAIN = 2.0
EPSILON = 1e-06


def extended_2(block, sides, width):
    for axis, dim in sides:
        count = lax.axis_size(axis)
        forward = [(i, i + 1) for i in range(count - 1)]
        forward.append((count - 1, 0))
        backward = [(target, source) for source, target in forward]
        low = lax.ppermute(
            lax.slice_in_dim(block, block.shape[dim] - width, None, axis=dim), axis, forward
        )
        high = lax.ppermute(lax.slice_in_dim(block, 0, width, axis=dim), axis, backward)
        block = jnp.concatenate([low, block, high], axis=dim)
    return block


def tracer_update(tracer, zonal_flow, merid_flow, wet_cells):
    face_x = wet_cells[:, :-1] * wet_cells[:, 1:]
    flow_x = 0.5 * (zonal_flow[:, :-1] + zonal_flow[:, 1:])
    west_vals = tracer[:, :, :-1]
    east_vals = tracer[:, :, 1:]
    flux_x = face_x * (
        0.5 * flow_x * (west_vals + east_vals) - DIFFUSIVITY * (east_vals - west_vals)
    )
    div_x = flux_x[:, :, 1:] - flux_x[:, :, :-1]
    interior = tracer[:, :, 1:-1]
    wet_mid = wet_cells[:, 1:-1]
    merid_mid = merid_flow[:, 1:-1]
    face_y = wet_mid[..., :-1] * wet_mid[..., 1:]
    flow_y = 0.5 * (merid_mid[..., :-1] + merid_mid[..., 1:])
    flux_y = face_y * (
        0.5 * flow_y * (interior[..., :-1] + interior[..., 1:])
        - DIFFUSIVITY * (interior[..., 1:] - interior[..., :-1])
    )
    padded = jnp.pad(flux_y, ((0, 0), (0, 0), (0, 0), (1, 1)))
    div_y = padded[..., 1:] - padded[..., :-1]
    return interior - TIME_STEP * (div_x + div_y)


def surface_operator(extended, face_x, face_y):
    grad_x = face_x * (extended[:, 1:] - extended[:, :-1])
    lap_x = grad_x[:, 1:] - grad_x[:, :-1]
    center = extended[:, 1:-1]
    grad_y = face_y * (center[..., 1:] - center[..., :-1])
    padded = jnp.pad(grad_y, ((0, 0), (0, 0), (1, 1)))
    lap_y = padded[..., 1:] - padded[..., :-1]
    return center - SURFACE_COUPLING * (lap_x + lap_y)


def apply_operator(surface, face_x, face_y):
    extended = extended_2(surface, (("lon", 1),), 1)
    return surface_operator(extended, face_x, face_y)


def local_products(lhs_field, rhs_field):
    return jnp.sum(lhs_field * rhs_field, axis=(1, 2))


def residual_squares(residual):
    return lax.psum(local_products(residual, residual), "lon")


def on_device(tracer_pert, surface_pert, zonal_flow, merid_flow, bottom_level):
    vectors, levels_count, columns, lat_rows = tracer_pert.shape
    levels = jnp.arange(levels_count, dtype=jnp.float32)[:, None, None]
    depths = bottom_level.astype(jnp.float32)
    wet_cells = (levels < depths[None]).astype(jnp.float32)
    tracer = wet_cells[None] * tracer_pert
    lead_rows = vectors * levels_count
    stacked = jnp.concatenate(
        [
            tracer.reshape(lead_rows, columns, lat_rows),
            surface_pert,
            zonal_flow,
            merid_flow,
            depths[None],
        ],
        axis=0,
    )
    extended = extended_2(stacked, (("lon", 1),), 1)
    tracer_ext = extended[:lead_rows].reshape(vectors, levels_count, columns + 2, lat_rows)
    zonal_ext = extended[lead_rows + vectors : lead_rows + vectors + levels_count]
    merid_ext = extended[
        lead_rows + vectors + levels_count : lead_rows + vectors + 2 * levels_count
    ]
    depth_ext = extended[-1]
    wet_ext = (levels < depth_ext[None]).astype(jnp.float32)
    tracer = tracer_update(tracer_ext, zonal_ext, merid_ext, wet_ext)
    refreshed = extended_2(tracer, (("lon", 2),), 1)
    tracer = tracer_update(refreshed, zonal_ext, merid_ext, wet_ext)
    surface_rim = extended[lead_rows : lead_rows + vectors]
    depth_rim = extended[-1]
    land_free = (depth_rim > 0).astype(jnp.float32)
    height_ext = surface_rim * land_free[None]
    face_x = jnp.minimum(depth_rim[:-1], depth_rim[1:])
    depth_mid = depth_rim[1:-1]
    face_y = jnp.minimum(depth_mid[:, :-1], depth_mid[:, 1:])
    height = height_ext[:, 1:-1]
    forcing = height + STERIC_GAIN * jnp.sum(tracer, axis=1) / levels_count
    residual = forcing - surface_operator(height_ext, face_x, face_y)
    solution = height
    direction = residual
    norm_now = residual_squares(residual)
    for iteration in range(ITERS):
        image_vec = apply_operator(direction, face_x, face_y)
        step_size = norm_now / lax.psum(local_products(direction, image_vec), "lon")
        solution = solution + step_size[:, None, None] * direction
        residual = residual - step_size[:, None, None] * image_vec
        if iteration + 1 < ITERS:
            norm_next = residual_squares(residual)
            direction = residual + (norm_next / norm_now)[:, None, None] * direction
            norm_now = norm_next
    cell_count = (levels_count + 1) * columns * lat_rows * lax.axis_size("lon")

    def local_inner(tracer_a, surface_a, tracer_b, surface_b):
        return (jnp.sum(tracer_a * tracer_b) + jnp.sum(surface_a * surface_b)) / cell_count

    first_tracer, second_tracer = (tracer[0], tracer[1])
    first_surface, second_surface = (solution[0], solution[1])
    gram_one, gram_mix, gram_two = lax.psum(
        (
            local_inner(first_tracer, first_surface, first_tracer, first_surface),
            local_inner(second_tracer, second_surface, first_tracer, first_surface),
            local_inner(second_tracer, second_surface, second_tracer, second_surface),
        ),
        "lon",
    )
    scale_one = jnp.sqrt(gram_one + EPSILON)
    cross = gram_mix / scale_one
    unit_tracer = first_tracer / scale_one
    unit_surface = first_surface / scale_one
    rest_tracer = second_tracer - cross * unit_tracer
    rest_surface = second_surface - cross * unit_surface
    rest_norm = gram_two - 2.0 * cross * cross + cross * cross * gram_one / (gram_one + EPSILON)
    scale_two = jnp.sqrt(rest_norm + EPSILON)
    tracer_vec = jnp.stack([unit_tracer, rest_tracer / scale_two])
    surface_vec = jnp.stack([unit_surface, rest_surface / scale_two])
    growth = jnp.stack([scale_one, cross, scale_two])
    return (tracer_vec, surface_vec, growth)


def solution(mesh):
    placed = (
        P("grp", None, "lon", None),
        P("grp", "lon", None),
        P(None, "lon", None),
        P(None, "lon", None),
        P("lon", None),
    )
    return jax.shard_map(
        on_device,
        mesh=mesh,
        in_specs=placed,
        out_specs=(P("grp", None, "lon", None), P("grp", "lon", None), P("grp")),
        check_vma=False,
    )
```

profile of v0, /device:TPU:0, one launch (start us, length us, event | category | flops | bytes accessed | tf_op | source)
XLA Modules:
  0.0 270.8 jit_solution(4647945465952432828)
XLA Ops:
  1.5 1.6 broadcast_multiply_fusion
  4.2 1.3 fusion.35
  5.6 5.5 %collective-permute-start.1 = (f32[203,1,1024]{2,0,1:T(8,128)S(1)}, f32[203,1,1024]{2,0,1:T(8,128)S(1)}, u32[]{:S(2)}, u32[]{:S(2)}) collective-permute-start(f32[203,1,1024]{2,0,1:T(8,128)S(1)} %copy.20), channel_id=1, source_target_pairs={{1,0},{2,1},{3,2},{4,3},{5,4},{6,5},{7,6},{8,7},{9,8},{10,9},{11,1... | collective-permute-start | bytes 2494472 | tf_op jit(solution)/shard_map/ppermute | solution.py:25
  12.1 9.2 %collective-permute-done.1 = f32[203,1,1024]{2,0,1:T(8,128)S(1)} collective-permute-done((f32[203,1,1024]{2,0,1:T(8,128)S(1)}, f32[203,1,1024]{2,0,1:T(8,128)S(1)}, u32[]{:S(2)}, u32[]{:S(2)}) %collective-permute-start.1) | collective-permute-done | bytes 831520 | tf_op jit(solution)/shard_map/ppermute | solution.py:25
  21.4 0.9 copy.22
  22.2 4.2 %collective-permute-done = f32[203,1,1024]{2,0,1:T(8,128)S(1)} collective-permute-done((f32[203,1,1024]{2,0,1:T(8,128)S(1)}, f32[203,1,1024]{2,0,1:T(8,128)S(1)}, u32[]{:S(2)}, u32[]{:S(2)}) %collective-permute-start) | collective-permute-done | bytes 831520 | tf_op jit(solution)/shard_map/ppermute | solution.py:22
  26.4 0.9 copy.21
  28.1 0.9 fusion.6
  29.0 2.6 pad_maximum_fusion
  31.7 1.5 subtract_multiply_fusion.3
  33.2 0.9 subtract_multiply_fusion.1
  34.1 1.5 fusion.5
  36.3 2.8 %collective-permute-start.2 = (f32[2,50,1,1024]{3,2,1,0:T(1,128)S(1)}, f32[2,50,1,1024]{3,2,1,0:T(1,128)S(1)}, u32[]{:S(2)}, u32[]{:S(2)}) collective-permute-start(f32[2,50,1,1024]{3,2,1,0:T(1,128)S(1)} %get-tuple-element.36), channel_id=1, source_target_pairs={{0,1},{1,2},{2,3},{3,4},{4,5},{5,6},{6,7},{7,8},{8,9},{9,10},{10,1... | collective-permute-start | bytes 1228808 | tf_op jit(solution)/shard_map/ppermute | solution.py:22
  39.0 1.7 collective-permute-start.3
  40.9 1.1 subtract_multiply_fusion.2
  42.0 4.5 %collective-permute-done.2 = f32[2,50,1,1024]{3,2,1,0:T(1,128)S(1)} collective-permute-done((f32[2,50,1,1024]{3,2,1,0:T(1,128)S(1)}, f32[2,50,1,1024]{3,2,1,0:T(1,128)S(1)}, u32[]{:S(2)}, u32[]{:S(2)}) %collective-permute-start.2) | collective-permute-done | bytes 409632 | tf_op jit(solution)/shard_map/ppermute | solution.py:22
  46.5 1.7 subtract_multiply_fusion
  48.3 1.5 fusion.33
  49.9 4.2 %collective-permute-start.5 = (f32[2,1,1024]{2,1,0:T(1,128)S(1)}, f32[2,1,1024]{2,1,0:T(1,128)S(1)}, u32[]{:S(2)}, u32[]{:S(2)}) collective-permute-start(f32[2,1,1024]{2,1,0:T(1,128)S(1)} %get-tuple-element.42), channel_id=1, source_target_pairs={{0,1},{1,2},{2,3},{3,4},{4,5},{5,6},{6,7},{7,8},{8,9},{9,10},{10,1... | collective-permute-start | bytes 24584 | tf_op jit(solution)/shard_map/ppermute | solution.py:22
  54.6 1.2 collective-permute-done.5
  56.4 33.5 %all-reduce.7 = (f32[2]{0:T(128)S(1)}, f32[2]{0:T(128)S(1)}) all-reduce(f32[2]{0:T(128)S(1)} %get-tuple-element.13, f32[2]{0:T(128)S(1)} %get-tuple-element.12), channel_id=1, replica_groups=mesh['grp'=2,'lon'=16] {'lon'}, use_global_device_ids=true, to_apply=%region_3.4 | all-reduce | flops 4 | bytes 32 | tf_op jit(solution)/shard_map/psum | solution.py:73
  90.1 29.5 %psum.65 = f32[2]{0:T(128)S(1)} all-reduce(f32[2]{0:T(128)S(1)} %get-tuple-element.27), channel_id=1, replica_groups=mesh['grp'=2,'lon'=16] {'lon'}, use_global_device_ids=true, to_apply=%region_7.8 | all-reduce | flops 2 | bytes 16 | tf_op jit(solution)/shard_map/psum | solution.py:73
  119.8 4.4 %collective-permute-start.6 = (f32[2,1,1024]{2,1,0:T(1,128)S(1)}, f32[2,1,1024]{2,1,0:T(1,128)S(1)}, u32[]{:S(2)}, u32[]{:S(2)}) collective-permute-start(f32[2,1,1024]{2,1,0:T(1,128)S(1)} %get-tuple-element.41), channel_id=1, source_target_pairs={{1,0},{2,1},{3,2},{4,3},{5,4},{6,5},{7,6},{8,7},{9,8},{10,9},{11,1... | collective-permute-start | bytes 24584 | tf_op jit(solution)/shard_map/ppermute | solution.py:25
  124.3 1.2 collective-permute-done.7
  125.8 33.9 %psum.66 = f32[2]{0:T(128)S(1)} all-reduce(f32[2]{0:T(128)S(1)} %get-tuple-element.25), channel_id=1, replica_groups=mesh['grp'=2,'lon'=16] {'lon'}, use_global_device_ids=true, to_apply=%region_9.10 | all-reduce | flops 2 | bytes 16 | tf_op jit(solution)/shard_map/psum | solution.py:119
  159.9 29.5 %psum.67 = f32[2]{0:T(128)S(1)} all-reduce(f32[2]{0:T(128)S(1)} %get-tuple-element.23), channel_id=1, replica_groups=mesh['grp'=2,'lon'=16] {'lon'}, use_global_device_ids=true, to_apply=%region_11.12 | all-reduce | flops 2 | bytes 16 | tf_op jit(solution)/shard_map/psum | solution.py:73
  189.5 4.4 %collective-permute-start.8 = (f32[2,1,1024]{2,1,0:T(1,128)S(1)}, f32[2,1,1024]{2,1,0:T(1,128)S(1)}, u32[]{:S(2)}, u32[]{:S(2)}) collective-permute-start(f32[2,1,1024]{2,1,0:T(1,128)S(1)} %get-tuple-element.39), channel_id=1, source_target_pairs={{1,0},{2,1},{3,2},{4,3},{5,4},{6,5},{7,6},{8,7},{9,8},{10,9},{11,1... | collective-permute-start | bytes 24584 | tf_op jit(solution)/shard_map/ppermute | solution.py:25
  194.0 1.2 collective-permute-done.9
  195.5 1.2 multiply_reduce_fusion.1
  196.8 33.9 %psum.68 = f32[2]{0:T(128)S(1)} all-reduce(f32[2]{0:T(128)S(1)} %fusion.12), channel_id=1, replica_groups=mesh['grp'=2,'lon'=16] {'lon'}, use_global_device_ids=true, to_apply=%region_13.14 | all-reduce | flops 2 | bytes 16 | tf_op jit(solution)/shard_map/psum | solution.py:119
  235.2 30.0 %all-reduce.6 = (f32[]{:T(128)}, f32[]{:T(128)}, f32[]{:T(128)}) all-reduce(f32[]{:T(128)S(6)} %div.73, f32[]{:T(128)S(6)} %div.78, f32[]{:T(128)S(6)} %div.76), channel_id=1, replica_groups=mesh['grp'=2,'lon'=16] {'lon'}, use_global_device_ids=true, to_apply=%region_15.16 | all-reduce | flops 3 | bytes 24 | tf_op jit(solution)/shard_map/psum | solution.py:133
  268.9 1.3 pad_maximum_fusion.3
  (64 shorter events, 9.6 us)
Async XLA Ops:
  1.5 1.7 copy-start.3
  1.5 1.7 copy-start.1
  3.1 1.0 copy-start
  3.1 1.1 copy-start.2
  5.6 15.7 %collective-permute-start.1 = (f32[203,1,1024]{2,0,1:T(8,128)S(1)}, f32[203,1,1024]{2,0,1:T(8,128)S(1)}, u32[]{:S(2)}, u32[]{:S(2)}) collective-permute-start(f32[203,1,1024]{2,0,1:T(8,128)S(1)} %copy.20), channel_id=1, source_target_pairs={{1,0},{2,1},{3,2},{4,3},{5,4},{6,5},{7,6},{8,7},{9,8},{10,9},{11,1... | collective-permute-start | bytes 2494472 | tf_op jit(solution)/shard_map/ppermute | solution.py:25
  11.3 15.1 %collective-permute-start = (f32[203,1,1024]{2,0,1:T(8,128)S(1)}, f32[203,1,1024]{2,0,1:T(8,128)S(1)}, u32[]{:S(2)}, u32[]{:S(2)}) collective-permute-start(f32[203,1,1024]{2,0,1:T(8,128)S(1)} %copy.19), channel_id=1, source_target_pairs={{0,1},{1,2},{2,3},{3,4},{4,5},{5,6},{6,7},{7,8},{8,9},{9,10},{10,1... | collective-permute-start | bytes 2494472 | tf_op jit(solution)/shard_map/ppermute | solution.py:22
  36.3 10.2 %collective-permute-start.2 = (f32[2,50,1,1024]{3,2,1,0:T(1,128)S(1)}, f32[2,50,1,1024]{3,2,1,0:T(1,128)S(1)}, u32[]{:S(2)}, u32[]{:S(2)}) collective-permute-start(f32[2,50,1,1024]{3,2,1,0:T(1,128)S(1)} %get-tuple-element.36), channel_id=1, source_target_pairs={{0,1},{1,2},{2,3},{3,4},{4,5},{5,6},{6,7},{7,8},{8,9},{9,10},{10,1... | collective-permute-start | bytes 1228808 | tf_op jit(solution)/shard_map/ppermute | solution.py:22
  39.0 7.5 %collective-permute-start.3 = (f32[2,50,1,1024]{3,2,1,0:T(1,128)S(1)}, f32[2,50,1,1024]{3,2,1,0:T(1,128)S(1)}, u32[]{:S(2)}, u32[]{:S(2)}) collective-permute-start(f32[2,50,1,1024]{3,2,1,0:T(1,128)S(1)} %get-tuple-element.37), channel_id=1, source_target_pairs={{1,0},{2,1},{3,2},{4,3},{5,4},{6,5},{7,6},{8,7},{9,8},{10,9},{11,1... | collective-permute-start | bytes 1228808 | tf_op jit(solution)/shard_map/ppermute | solution.py:25
  49.9 5.8 %collective-permute-start.5 = (f32[2,1,1024]{2,1,0:T(1,128)S(1)}, f32[2,1,1024]{2,1,0:T(1,128)S(1)}, u32[]{:S(2)}, u32[]{:S(2)}) collective-permute-start(f32[2,1,1024]{2,1,0:T(1,128)S(1)} %get-tuple-element.42), channel_id=1, source_target_pairs={{0,1},{1,2},{2,3},{3,4},{4,5},{5,6},{6,7},{7,8},{8,9},{9,10},{10,1... | collective-permute-start | bytes 24584 | tf_op jit(solution)/shard_map/ppermute | solution.py:22
  54.1 2.1 collective-permute-start.4
  119.7 5.8 %collective-permute-start.7 = (f32[2,1,1024]{2,1,0:T(1,128)S(1)}, f32[2,1,1024]{2,1,0:T(1,128)S(1)}, u32[]{:S(2)}, u32[]{:S(2)}) collective-permute-start(f32[2,1,1024]{2,1,0:T(1,128)S(1)} %get-tuple-element.40), channel_id=1, source_target_pairs={{0,1},{1,2},{2,3},{3,4},{4,5},{5,6},{6,7},{7,8},{8,9},{9,10},{10,1... | collective-permute-start | bytes 24584 | tf_op jit(solution)/shard_map/ppermute | solution.py:22
  119.8 5.8 %collective-permute-start.6 = (f32[2,1,1024]{2,1,0:T(1,128)S(1)}, f32[2,1,1024]{2,1,0:T(1,128)S(1)}, u32[]{:S(2)}, u32[]{:S(2)}) collective-permute-start(f32[2,1,1024]{2,1,0:T(1,128)S(1)} %get-tuple-element.41), channel_id=1, source_target_pairs={{1,0},{2,1},{3,2},{4,3},{5,4},{6,5},{7,6},{8,7},{9,8},{10,9},{11,1... | collective-permute-start | bytes 24584 | tf_op jit(solution)/shard_map/ppermute | solution.py:25
  189.4 5.8 %collective-permute-start.9 = (f32[2,1,1024]{2,1,0:T(1,128)S(1)}, f32[2,1,1024]{2,1,0:T(1,128)S(1)}, u32[]{:S(2)}, u32[]{:S(2)}) collective-permute-start(f32[2,1,1024]{2,1,0:T(1,128)S(1)} %get-tuple-element.38), channel_id=1, source_target_pairs={{0,1},{1,2},{2,3},{3,4},{4,5},{5,6},{6,7},{7,8},{8,9},{9,10},{10,1... | collective-permute-start | bytes 24584 | tf_op jit(solution)/shard_map/ppermute | solution.py:22
  189.5 5.8 %collective-permute-start.8 = (f32[2,1,1024]{2,1,0:T(1,128)S(1)}, f32[2,1,1024]{2,1,0:T(1,128)S(1)}, u32[]{:S(2)}, u32[]{:S(2)}) collective-permute-start(f32[2,1,1024]{2,1,0:T(1,128)S(1)} %get-tuple-element.39), channel_id=1, source_target_pairs={{1,0},{2,1},{3,2},{4,3},{5,4},{6,5},{7,6},{8,7},{9,8},{10,9},{11,1... | collective-permute-start | bytes 24584 | tf_op jit(solution)/shard_map/ppermute | solution.py:25
where the time goes:
time: 271 us
  blocking collectives  190 us (70%)
  starting transfers between devices  23.8 us (9%)
  waiting for transfers between devices  22.2 us (8%)
  other arithmetic  21.9 us (8%)
  between operations  7.55 us (3%)
  local copies, waits for them, and re-layouts  5.13 us (2%)
    psum x3, blocking collectives, residual_squares(): return lax.psum(local_products(residual, residual), 'lon')  92.5 us
    psum x2, blocking collectives, on_device(): step_size = norm_now / lax.psum(local_products(direction, image_vec), 'lon')  67.8 us
    psum x1, blocking collectives, on_device(): lax.psum((local_inner(first_tracer, first_surface, first_tracer, first_su...  30 us
    ppermute x5, starting transfers between devices, extended_2(): lax.ppermute(lax.slice_in_dim(block, 0, width, axis=dim), axis, backward)  16.5 us
    ppermute x5, waiting for transfers between devices, extended_2(): lax.ppermute(lax.slice_in_dim(block, block.shape[dim] - width, None, axis...  12.4 us
    ppermute x5, waiting for transfers between devices, extended_2(): lax.ppermute(lax.slice_in_dim(block, 0, width, axis=dim), axis, backward)  9.78 us
    ppermute x5, starting transfers between devices, extended_2(): lax.ppermute(lax.slice_in_dim(block, block.shape[dim] - width, None, axis...  7.28 us
  transfers between devices with their start and end apart: 10, of which 7 were waited for; matrix products, arithmetic and copies ran while one was open for 1% of the time, Pallas kernels for 0%

commit v1 on v0

v1 whole, which is shorter than its diff:
```python
import functools

import jax
import jax.numpy as jnp
from jax import lax
from jax.experimental import pallas as pl
from jax.experimental.pallas import tpu as pltpu
from jax.sharding import PartitionSpec as P

DIFFUSIVITY = 0.5
TIME_STEP = 0.2
SURFACE_COUPLING = 0.5
STERIC_GAIN = 2.0
EPSILON = 1e-06
MESH = pl.DeviceIdType.MESH
CHUNKS = 5
UNROLL = 2
REACH = 2


def chunk_bounds(levels):
    count = min(CHUNKS, levels)
    edges = [levels * i // count for i in range(count + 1)]
    return list(zip(edges[:-1], edges[1:]))


def peers_loop(n, body):
    if n <= 16:
        for i in range(1, n):
            body(i)
    else:

        def step(i, carry):
            body(i)
            return carry

        lax.fori_loop(1, n, step, 0)


def kernel(
    n, trc, surf, zon, mer, bot, out, sout, gout,
    s_a, r_a, s_b, r_b, coef, stat, ster, pack, red,
    a_send, a_recv, b_send, b_recv, st_send, st_recv, se_send, se_recv, rd_send, rd_recv,
):
    me = lax.axis_index("lon")
    levels = zon.shape[0]
    chunks = chunk_bounds(levels)
    right, left = lax.rem(me + 1, n), lax.rem(me + n - 1, n)
    side_dev = (left, right)
    tile = (8, 128)
    lane = lax.broadcasted_iota(jnp.int32, tile, 1)
    row = lax.broadcasted_iota(jnp.int32, tile, 0)
    last_lane, first_lane = lane == 127, lane == 0

    def north(x):
        rolled = pltpu.roll(x, 127, 1)
        return jnp.where(last_lane, pltpu.roll(rolled, 7, 0), rolled)

    def south(x):
        rolled = pltpu.roll(x, 1, 1)
        return jnp.where(first_lane, pltpu.roll(rolled, 1, 0), rolled)

    def col(c):
        return pl.ds(c, 8, stride=2)

    barrier = pltpu.get_barrier_semaphore()

    def greet(i):
        pl.semaphore_signal(
            barrier, inc=1, device_id={"lon": lax.rem(me + i, n)}, device_id_type=MESH
        )

    peers_loop(n, greet)

    for c in range(2):
        d = bot[col(c), :].astype(jnp.float32)
        stat[REACH, 4 + c] = d
        for v in range(2):
            stat[REACH, 2 * v + c] = jnp.where(d > 0, surf[v, col(c), :], 0.0)

    def gather_chunk(k0, k1):
        def step(k, carry):
            for c in range(2):
                s_a[c, k, 0] = trc[0, k, col(c), :]
                s_a[c, k, 1] = trc[1, k, col(c), :]
                s_a[c, k, 2] = zon[k, col(c), :]
            return carry

        lax.fori_loop(k0, k1, step, 0, unroll=UNROLL)

    def a_copy(g, side):
        k0, k1 = chunks[g]
        return pltpu.make_async_remote_copy(
            src_ref=s_a.at[side, pl.ds(k0, k1 - k0)],
            dst_ref=r_a.at[1 - side, pl.ds(k0, k1 - k0)],
            send_sem=a_send.at[side, g],
            recv_sem=a_recv.at[1 - side, g],
            device_id={"lon": side_dev[side]},
            device_id_type=MESH,
        )

    def b_copy(g, side):
        k0, k1 = chunks[g]
        return pltpu.make_async_remote_copy(
            src_ref=s_b.at[side, pl.ds(k0, k1 - k0)],
            dst_ref=r_b.at[1 - side, pl.ds(k0, k1 - k0)],
            send_sem=b_send.at[side, g],
            recv_sem=b_recv.at[1 - side, g],
            device_id={"lon": side_dev[side]},
            device_id_type=MESH,
        )

    shifts = [s for s in range(-REACH, REACH + 1) if s != 0]
    shifts.sort(key=abs)

    def halo_copy(buf, send, recv, s):
        return pltpu.make_async_remote_copy(
            src_ref=buf.at[REACH],
            dst_ref=buf.at[REACH - s],
            send_sem=send.at[REACH - s],
            recv_sem=recv.at[REACH - s],
            device_id={"lon": lax.rem(me + s + n, n)},
            device_id_type=MESH,
        )

    gather_chunk(*chunks[0])
    pl.semaphore_wait(barrier, n - 1)
    for s in shifts:
        halo_copy(stat, st_send, st_recv, s).start()
    for side in range(2):
        a_copy(0, side).start()
    for g in range(1, len(chunks)):
        gather_chunk(*chunks[g])
        for side in range(2):
            a_copy(g, side).start()

    for s in shifts:
        halo_copy(stat, st_send, st_recv, s).wait_recv()
    width = 2 * (2 * REACH + 1)
    mid = 2 * REACH

    def depth(i):
        return stat[i // 2, 4 + i % 2]

    def height(v, i):
        return stat[i // 2, 2 * v + i % 2]

    def y_face(i):
        d = depth(i)
        wall = jnp.logical_and(last_lane, row == 7)
        return jnp.where(wall, 0.0, jnp.minimum(d, north(d)))

    def x_face(i):
        return jnp.minimum(depth(i), depth(i + 1))

    half = TIME_STEP * 0.25
    diff = TIME_STEP * DIFFUSIVITY

    for g, (k0, k1) in enumerate(chunks):
        for side in range(2):
            a_copy(g, side).wait_recv()

        def first(k, carry):
            kf = k.astype(jnp.float32)
            z = (r_a[0, k, 2], s_a[0, k, 2], s_a[1, k, 2], r_a[1, k, 2])
            cx = []
            for f in range(3):
                open_f = kf < x_face(mid - 1 + f)
                u = half * (z[f] + z[f + 1])
                cx.append((jnp.where(open_f, u + diff, 0.0), jnp.where(open_f, u - diff, 0.0)))
            cy = []
            for c in range(2):
                open_f = kf < faces_y[c]
                m = mer[k, col(c), :]
                u = half * (m + north(m))
                cy.append((jnp.where(open_f, u + diff, 0.0), jnp.where(open_f, u - diff, 0.0)))
            for q, (lo, hi) in enumerate(cx + cy):
                coef[k, 2 * q] = lo
                coef[k, 2 * q + 1] = hi
            wet = [kf < depth(mid + c) for c in range(2)]
            for v in range(2):
                t = (
                    r_a[0, k, v],
                    jnp.where(wet[0], s_a[0, k, v], 0.0),
                    jnp.where(wet[1], s_a[1, k, v], 0.0),
                    r_a[1, k, v],
                )
                fx = [cx[f][0] * t[f] + cx[f][1] * t[f + 1] for f in range(3)]
                for c in range(2):
                    fy = cy[c][0] * t[c + 1] + cy[c][1] * north(t[c + 1])
                    s_b[c, k, v] = t[c + 1] - ((fx[c + 1] - fx[c]) + (fy - south(fy)))
            return carry

        if g == 0:
            faces_y = [y_face(mid + c) for c in range(2)]
        lax.fori_loop(k0, k1, first, 0, unroll=UNROLL)
        for side in range(2):
            b_copy(g, side).start()

    face_x = {i: SURFACE_COUPLING * x_face(i) for i in range(0, width - 1)}
    face_y = {i: SURFACE_COUPLING * y_face(i) for i in range(1, width - 1)}

    def lap(s, cols):
        gx = {i: face_x[i] * (s[i + 1] - s[i]) for i in range(cols[0] - 1, cols[-1] + 1)}
        res = {}
        for i in cols:
            gy = face_y[i] * (north(s[i]) - s[i])
            res[i] = -((gx[i] - gx[i - 1]) + (gy - south(gy)))
        return res

    lap_h = [
        lap({i: height(v, i) for i in range(width)}, range(1, width - 1)) for v in range(2)
    ]

    zero = jnp.zeros(tile, jnp.float32)
    totals = (zero,) * 7
    for g, (k0, k1) in enumerate(chunks):
        for side in range(2):
            b_copy(g, side).wait_recv()

        def second(k, carry):
            sums, grams = list(carry[:4]), list(carry[4:])
            cx = [(coef[k, 2 * f], coef[k, 2 * f + 1]) for f in range(3)]
            cy = [(coef[k, 6 + 2 * c], coef[k, 7 + 2 * c]) for c in range(2)]
            new = []
            for v in range(2):
                t = (r_b[0, k, v], s_b[0, k, v], s_b[1, k, v], r_b[1, k, v])
                fx = [cx[f][0] * t[f] + cx[f][1] * t[f + 1] for f in range(3)]
                for c in range(2):
                    fy = cy[c][0] * t[c + 1] + cy[c][1] * north(t[c + 1])
                    val = t[c + 1] - ((fx[c + 1] - fx[c]) + (fy - south(fy)))
                    out[v, k, col(c), :] = val
                    sums[2 * v + c] = sums[2 * v + c] + val
                    new.append(val)
            grams[0] = grams[0] + (new[0] * new[0] + new[1] * new[1])
            grams[1] = grams[1] + (new[0] * new[2] + new[1] * new[3])
            grams[2] = grams[2] + (new[2] * new[2] + new[3] * new[3])
            return tuple(sums + grams)

        totals = lax.fori_loop(k0, k1, second, totals, unroll=UNROLL)

    for q in range(4):
        ster[REACH, q] = totals[q]
    for s in shifts:
        halo_copy(ster, se_send, se_recv, s).start()

    def total_of(x):
        return jnp.sum(jnp.sum(x, axis=1, keepdims=True), axis=0, keepdims=True)

    def red_copy(turn, i):
        return pltpu.make_async_remote_copy(
            src_ref=pack.at[turn],
            dst_ref=red.at[turn, me],
            send_sem=rd_send.at[turn],
            recv_sem=rd_recv.at[turn],
            device_id={"lon": lax.rem(me + i, n)},
            device_id_type=MESH,
        )

    def all_sum(turn, parts):
        mine = zero
        for q, part in enumerate(parts):
            mine = jnp.where(lane == q, total_of(part), mine)
        pack[turn] = mine
        red[turn, me] = mine
        peers_loop(n, lambda i: red_copy(turn, i).start())
        every = pltpu.make_async_copy(
            red.at[turn, pl.ds(0, n - 1)], red.at[turn, pl.ds(0, n - 1)], rd_recv.at[turn]
        )
        every.wait()
        terms = [red[turn, i] for i in range(n)]
        while len(terms) > 1:
            terms = [
                terms[i] + terms[i + 1] if i + 1 < len(terms) else terms[i]
                for i in range(0, len(terms), 2)
            ]
        return [terms[0][0:1, q : q + 1] for q in range(len(parts))]

    gram_parts = list(totals[4:])
    for s in shifts:
        halo_copy(ster, se_send, se_recv, s).wait_recv()

    own = (mid, mid + 1)

    def dot(a, b):
        return a[own[0]] * b[own[0]] + a[own[1]] * b[own[1]]

    gain = STERIC_GAIN / levels
    res, lres, llres, parts = [], [], [], []
    for v in range(2):
        r = {
            i: gain * ster[i // 2, 2 * v + i % 2] - lap_h[v][i] for i in range(1, width - 1)
        }
        lr = lap(r, range(2, width - 2))
        llr = lap(lr, range(own[0], own[1] + 1))
        res.append(r)
        lres.append(lr)
        parts += [dot(r, r), dot(r, lr), dot(lr, lr), dot(lr, llr)]
    sums = all_sum(0, parts + gram_parts)
    gram_t = sums[8:]

    sol, dir1, res2, rr1s, parts = [], [], [], [], []
    ldir1s = []
    for v in range(2):
        l0, l1, l2, l3 = sums[4 * v : 4 * v + 4]
        step0 = l0 / (l0 + l1)
        ratio = l1 / l0
        rr1 = step0 * step0 * jnp.maximum(l2 - l1 * ratio, 0.0)
        beta0 = rr1 / l0
        along = step0 * ratio + beta0
        p1ap1 = (
            along * along * (l0 + l1)
            - 2.0 * along * step0 * (l1 + l2)
            + step0 * step0 * (l2 + l3)
        )
        step1 = rr1 / p1ap1
        r, lr = res[v], lres[v]
        p1 = {i: along * r[i] - step0 * lr[i] for i in range(own[0] - 2, own[1] + 3)}
        lp1 = lap(p1, range(own[0] - 1, own[1] + 2))
        r2 = {
            i: step0 * (ratio * r[i] - lr[i]) - step1 * (p1[i] + lp1[i])
            for i in range(own[0] - 1, own[1] + 2)
        }
        lr2 = lap(r2, range(own[0], own[1] + 1))
        s = {i: height(v, i) + (step0 * r[i] + step1 * p1[i]) for i in own}
        parts += [dot(r2, lr2), dot(r2, lp1), dot(p1, lp1)]
        parts += [dot(s, s), dot(s, r2), dot(s, p1), dot(r2, r2), dot(r2, p1), dot(p1, p1)]
        sol.append(s)
        dir1.append(p1)
        res2.append(r2)
        rr1s.append(rr1)
    for a in (sol[0], res2[0], dir1[0]):
        for b in (sol[1], res2[1], dir1[1]):
            parts.append(dot(a, b))
    sums = all_sum(1, parts)
    weights, final = [], []
    for v in range(2):
        r2lr2, r2lp1, p1lp1, ss, sr, sp, rr2, rp, pp = sums[9 * v : 9 * v + 9]
        beta1 = rr2 / rr1s[v]
        p2ap2 = (
            (rr2 + r2lr2) + 2.0 * beta1 * (rp + r2lp1) + beta1 * beta1 * (pp + p1lp1)
        )
        step2 = rr2 / p2ap2
        e, f = step2, step2 * beta1
        weights.append((e, f))
        final.append(
            ss + 2.0 * (e * sr + f * sp) + (e * e * rr2 + 2.0 * e * f * rp + f * f * pp)
        )
        for c in range(2):
            i = own[c]
            sout[v, col(c), :] = sol[v][i] + (e * res2[v][i] + f * dir1[v][i])
    cross_parts = sums[18:]
    (e0, f0), (e1, f1) = weights
    wa, wb = (None, e0, f0), (None, e1, f1)
    mix = cross_parts[0]
    for i in range(3):
        for j in range(3):
            if i == 0 and j == 0:
                continue
            term = cross_parts[3 * i + j]
            if wa[i] is not None:
                term = term * wa[i]
            if wb[j] is not None:
                term = term * wb[j]
            mix = mix + term
    count = float((levels + 1) * 2 * 8 * 128 * n)
    gram_one = (gram_t[0] + final[0]) / count
    gram_mix = (gram_t[1] + mix) / count
    gram_two = (gram_t[2] + final[1]) / count
    scale_one = jnp.sqrt(gram_one + EPSILON)
    cross = gram_mix / scale_one
    rest = gram_two - 2.0 * cross * cross + cross * cross * gram_one / (gram_one + EPSILON)
    scale_two = jnp.sqrt(rest + EPSILON)
    growth = jnp.where(lane == 0, scale_one, jnp.where(lane == 1, cross, scale_two))
    gout[...] = growth

    for g in range(len(chunks)):
        for side in range(2):
            a_copy(g, side).wait_send()
            b_copy(g, side).wait_send()
    for s in shifts:
        halo_copy(stat, st_send, st_recv, s).wait_send()
        halo_copy(ster, se_send, se_recv, s).wait_send()
    for turn in range(2):
        pltpu.make_async_copy(
            red.at[turn, pl.ds(0, n - 1)], red.at[turn, pl.ds(0, n - 1)], rd_send.at[turn]
        ).wait()


def packed(x):
    lead, (cols, rows) = x.shape[:-2], x.shape[-2:]
    x = x.reshape(lead + (cols, rows // 128, 128))
    x = jnp.swapaxes(x, -3, -2)
    return x.reshape(lead + (cols * (rows // 128), 128))


def unpacked(x, cols):
    lead, (rows, lanes) = x.shape[:-2], x.shape[-2:]
    x = x.reshape(lead + (rows // cols, cols, lanes))
    x = jnp.swapaxes(x, -3, -2)
    return x.reshape(lead + (cols, rows // cols * lanes))


def on_device(n, tracer_pert, surface_pert, zonal_flow, merid_flow, bottom_level):
    vectors, levels, columns, rows = tracer_pert.shape
    count = len(chunk_bounds(levels))
    f32 = jnp.float32
    vmem = pl.BlockSpec(memory_space=pltpu.VMEM)
    dma = pltpu.SemaphoreType.DMA
    slots = 2 * REACH + 1
    tracer, surface, tail = pl.pallas_call(
        functools.partial(kernel, n),
        out_shape=(
            jax.ShapeDtypeStruct((vectors, levels, 16, 128), f32),
            jax.ShapeDtypeStruct((vectors, 16, 128), f32),
            jax.ShapeDtypeStruct((8, 128), f32),
        ),
        in_specs=[vmem] * 5,
        out_specs=(vmem,) * 3,
        scratch_shapes=[
            pltpu.VMEM((2, levels, 3, 8, 128), f32),
            pltpu.VMEM((2, levels, 3, 8, 128), f32),
            pltpu.VMEM((2, levels, 2, 8, 128), f32),
            pltpu.VMEM((2, levels, 2, 8, 128), f32),
            pltpu.VMEM((levels, 10, 8, 128), f32),
            pltpu.VMEM((slots, 6, 8, 128), f32),
            pltpu.VMEM((slots, 4, 8, 128), f32),
            pltpu.VMEM((2, 8, 128), f32),
            pltpu.VMEM((2, n, 8, 128), f32),
            dma((2, count)),
            dma((2, count)),
            dma((2, count)),
            dma((2, count)),
            dma((slots,)),
            dma((slots,)),
            dma((slots,)),
            dma((slots,)),
            dma((2,)),
            dma((2,)),
        ],
        compiler_params=pltpu.CompilerParams(
            collective_id=0, has_side_effects=True, vmem_limit_bytes=40 * 1024 * 1024
        ),
    )(
        packed(tracer_pert),
        packed(surface_pert),
        packed(zonal_flow),
        packed(merid_flow),
        packed(bottom_level),
    )
    growth = tail[0, :3]
    scale_one, cross, scale_two = growth[0], growth[1], growth[2]

    def renormalized(x):
        unit = x[0] / scale_one
        rest = (x[1] - cross * unit) / scale_two
        return unpacked(jnp.stack([unit, rest]), columns)

    return renormalized(tracer), renormalized(surface), growth


def solution(mesh):
    placed = (
        P("grp", None, "lon", None),
        P("grp", "lon", None),
        P(None, "lon", None),
        P(None, "lon", None),
        P("lon", None),
    )
    return jax.shard_map(
        functools.partial(on_device, mesh.shape["lon"]),
        mesh=mesh,
        in_specs=placed,
        out_specs=(P("grp", None, "lon", None), P("grp", "lon", None), P("grp")),
        check_vma=False,
    )
```

time: 271 us -> 58.8 us (0.22)
  blocking collectives: 190 us -> 0 us
  Pallas kernels: 0 us -> 46.1 us
  starting transfers between devices: 23.8 us -> 0 us
  waiting for transfers between devices: 22.2 us -> 0 us
  other arithmetic: 21.9 us -> 5.95 us
  between operations: 7.55 us -> 0.67 us
    psum x6 -> x0, blocking collectives: 190 us -> none  [the longest x3 92.5 us: residual_squares(): return lax.psum(local_products(residual, residual), 'lon')]
    pallas_call x0 -> x1, Pallas kernels: none -> 46.1 us  [on_device(): pl.pallas_call(functools.partial(kernel, n), out_shape=(jax.ShapeDtypeStr...]
    ppermute x10 -> x0, starting transfers between devices: 23.8 us -> none  [the longest x5 16.5 us: extended_2(): lax.ppermute(lax.slice_in_dim(block, 0, width, axis=dim), axis, backward)]
    ppermute x10 -> x0, waiting for transfers between devices: 22.2 us -> none  [the longest x5 12.4 us: extended_2(): lax.ppermute(lax.slice_in_dim(block, block.shape[dim] - width, None, axis...]
    mul x19 -> x0, other arithmetic: 9.15 us -> none  [the longest x2 2.62 us: tracer_update(): face_x * (0.5 * flow_x * (west_vals + east_vals) - DIFFUSIVITY * (east_va...]
    reduce_sum x8 -> x0, other arithmetic: 4.36 us -> none  [the longest x1 1.54 us: on_device(): forcing = height + STERIC_GAIN * jnp.sum(tracer, axis=1) / levels_count]
    div x7 -> x2, other arithmetic: 0.34 us -> 4.03 us  [renormalized(): rest = (x[1] - cross * unit) / scale_two]
    unnamed x12 -> x10, local copies, waits for them, and re-layouts: 1.02 us -> 4.55 us
  transfers between devices with their start and end apart: 10 -> 0, of which waited for: 7 -> 0; matrix products, arithmetic and copies ran while one was open for 1% -> 0% of each run, Pallas kernels for 0% -> 0%
where the time goes in v1:
time: 58.8 us; the launch traced here: 58.4 us
  Pallas kernels  46.1 us (78%)
  other arithmetic  5.95 us (10%)
  local copies, waits for them, and re-layouts  5.72 us (10%)
  between operations  0.67 us (1%)
    pallas_call x1, Pallas kernels, on_device(): pl.pallas_call(functools.partial(kernel, n), out_shape=(jax.ShapeDtypeStr...  46.1 us
    unnamed x10, local copies, waits for them, and re-layouts  4.55 us
    div x2, other arithmetic, renormalized(): rest = (x[1] - cross * unit) / scale_two  4.03 us
    reshape x2, other arithmetic, unpacked(): return x.reshape(lead + (cols, rows // cols * lanes))  1.93 us

profile of v1, /device:TPU:0, one launch (start us, length us, event | category | flops | bytes accessed | tf_op | source)
XLA Modules:
  0.0 58.4 jit_solution(3918003143557932362)
XLA Ops:
  0.6 0.0 copy-start.4
  0.6 0.7 %copy-done.4 = s32[2,1024]{1,0:T(2,128)S(1)} copy-done((s32[2,1024]{1,0:T(2,128)S(1)}, s32[2,1024]{1,0:T(2,128)}, u32[]{:S(2)}) %copy-start.4) | copy-done | bytes 8216
  1.3 0.0 copy-start
  1.3 1.1 %copy-done = f32[2,50,2,1024]{3,2,1,0:T(2,128)S(1)} copy-done((f32[2,50,2,1024]{3,2,1,0:T(2,128)S(1)}, f32[2,50,2,1024]{3,2,1,0:T(2,128)}, u32[]{:S(2)}) %copy-start) | copy-done | bytes 819224
  2.5 0.0 copy-start.1
  2.5 1.0 %copy-done.1 = f32[50,2,1024]{2,1,0:T(2,128)S(1)} copy-done((f32[50,2,1024]{2,1,0:T(2,128)S(1)}, f32[50,2,1024]{2,1,0:T(2,128)}, u32[]{:S(2)}) %copy-start.1) | copy-done | bytes 409624
  3.5 0.0 copy-start.2
  3.5 1.0 %copy-done.2 = f32[50,2,1024]{2,1,0:T(2,128)S(1)} copy-done((f32[50,2,1024]{2,1,0:T(2,128)S(1)}, f32[50,2,1024]{2,1,0:T(2,128)}, u32[]{:S(2)}) %copy-start.2) | copy-done | bytes 409624
  4.5 0.0 copy-start.3
  4.5 0.7 %copy-done.3 = f32[2,2,1024]{2,1,0:T(2,128)S(1)} copy-done((f32[2,2,1024]{2,1,0:T(2,128)S(1)}, f32[2,2,1024]{2,1,0:T(2,128)}, u32[]{:S(2)}) %copy-start.3) | copy-done | bytes 16408
  5.2 46.1 %shard_map.76 = (f32[2,50,16,128]{3,2,1,0:T(8,128)S(1)}, f32[2,16,128]{2,1,0:T(8,128)S(1)}, f32[8,128]{1,0:T(8,128)S(1)}) custom-call(f32[2,50,16,128]{3,2,1,0:T(8,128)S(1)} %bitcast.42, f32[2,16,128]{2,1,0:T(8,128)S(1)} %bitcast.45, f32[50,16,128]{2,1,0:T(8,128)S(1)} %bitcast.43, f32[50,16,128]{2,1,0:T(8,128)S(1)} %bitcast.44, s32[16,128]{1,0:T(8,128)S(1)} %bitcast.46), custom_call_target="tpu_custom_call" | custom-call | tf_op jit(solution)/shard_map/pallas_call | solution.py:411
  51.3 0.5 slice_bitcast_fusion
  51.8 0.7 %fusion = (f32[1,1]{1,0:T(1,128)}, f32[1,1]{1,0:T(1,128)}, f32[1,1]{1,0:T(1,128)}) fusion(f32[8,128]{1,0:T(8,128)S(1)} %get-tuple-element.7), kind=kLoop, calls=%fused_computation.7 | loop fusion | bytes 24 | tf_op jit(solution)/shard_map/slice | solution.py:452
  52.4 2.0 %subtract_divide_fusion.1 = (f32[1,16,128]{2,1,0:T(8,128)S(1)}, f32[1,16,128]{2,1,0:T(8,128)S(1)}) fusion(f32[2,16,128]{2,1,0:T(8,128)S(1)} %get-tuple-element.8, f32[]{:T(128)} %bitcast.18, f32[]{:T(128)} %bitcast.17, f32[]{:T(128)} %bitcast.15), kind=kLoop, calls=%fused_computation.4 | loop fusion | flops 8192 | bytes 32780 | tf_op jit(solution)/shard_map/div | solution.py:456
  54.4 2.0 %subtract_divide_fusion = (f32[1,50,16,128]{3,2,1,0:T(8,128)S(1)}, f32[1,50,16,128]{3,2,1,0:T(8,128)S(1)}) fusion(f32[2,50,16,128]{3,2,1,0:T(8,128)S(1)} %get-tuple-element.6, f32[]{:T(128)} %bitcast.18, f32[]{:T(128)} %bitcast.17, f32[]{:T(128)} %bitcast.15), kind=kLoop, calls=%fused_computation.1 | loop fusion | flops 409600 | bytes 1638412 | tf_op jit(solution)/shard_map/div | solution.py:456
  56.5 1.3 %maximum_bitcast_fusion = f32[2,50,2,1024]{3,2,1,0:T(2,128)} fusion(f32[1,50,8,2,128]{4,3,2,1,0:T(2,128)S(1)} %bitcast.47, f32[1,50,8,2,128]{4,3,2,1,0:T(2,128)S(1)} %bitcast.48), kind=kLoop, calls=%fused_computation | loop fusion | flops 204800 | bytes 1638400 | tf_op jit(solution)/shard_map/reshape | solution.py:401
  57.8 0.6 %maximum_bitcast_fusion.1 = f32[2,2,1024]{2,1,0:T(2,128)} fusion(f32[1,8,2,128]{3,2,1,0:T(2,128)S(1)} %bitcast.49, f32[1,8,2,128]{3,2,1,0:T(2,128)S(1)} %bitcast.50), kind=kLoop, calls=%fused_computation.3 | loop fusion | flops 4096 | bytes 32768 | tf_op jit(solution)/shard_map/reshape | solution.py:401
Async XLA Ops:
  0.6 0.7 %copy-start.4 = (s32[2,1024]{1,0:T(2,128)S(1)}, s32[2,1024]{1,0:T(2,128)}, u32[]{:S(2)}) copy-start(s32[2,1024]{1,0:T(2,128)} %param.9) | copy-start | bytes 24580
  1.3 1.1 %copy-start = (f32[2,50,2,1024]{3,2,1,0:T(2,128)S(1)}, f32[2,50,2,1024]{3,2,1,0:T(2,128)}, u32[]{:S(2)}) copy-start(f32[2,50,2,1024]{3,2,1,0:T(2,128)} %param.5) | copy-start | bytes 2457604
  2.5 1.0 %copy-start.1 = (f32[50,2,1024]{2,1,0:T(2,128)S(1)}, f32[50,2,1024]{2,1,0:T(2,128)}, u32[]{:S(2)}) copy-start(f32[50,2,1024]{2,1,0:T(2,128)} %param.7) | copy-start | bytes 1228804
  3.5 1.0 %copy-start.2 = (f32[50,2,1024]{2,1,0:T(2,128)S(1)}, f32[50,2,1024]{2,1,0:T(2,128)}, u32[]{:S(2)}) copy-start(f32[50,2,1024]{2,1,0:T(2,128)} %param.8) | copy-start | bytes 1228804
  4.5 0.7 %copy-start.3 = (f32[2,2,1024]{2,1,0:T(2,128)S(1)}, f32[2,2,1024]{2,1,0:T(2,128)}, u32[]{:S(2)}) copy-start(f32[2,2,1024]{2,1,0:T(2,128)} %param.6) | copy-start | bytes 49156

commit v2 on v1

--- a/solution.py
+++ b/solution.py
@@ -38,12 +38,12 @@
 
 
 def kernel(
-    n, trc, surf, zon, mer, bot, out, sout, gout,
-    s_a, r_a, s_b, r_b, coef, stat, ster, pack, red,
+    n, trc_hbm, surf_hbm, zon_hbm, mer_hbm, bot_hbm, out, sout, gout,
+    trc, surf, zon, mer, bot, in_sem, few_sem, s_a, r_a, s_b, r_b, coef, stat, ster, pack, red,
     a_send, a_recv, b_send, b_recv, st_send, st_recv, se_send, se_recv, rd_send, rd_recv,
 ):
     me = lax.axis_index("lon")
-    levels = zon.shape[0]
+    levels = zon_hbm.shape[0]
     chunks = chunk_bounds(levels)
     right, left = lax.rem(me + 1, n), lax.rem(me + n - 1, n)
     side_dev = (left, right)
@@ -63,6 +63,26 @@
     def col(c):
         return pl.ds(c, 8, stride=2)
 
+    def in_copies(g):
+        k0, k1 = chunks[g]
+        ks = pl.ds(k0, k1 - k0)
+        return (
+            pltpu.make_async_copy(trc_hbm.at[:, ks], trc.at[:, ks], in_sem.at[g, 0]),
+            pltpu.make_async_copy(zon_hbm.at[ks], zon.at[ks], in_sem.at[g, 1]),
+        )
+
+    bot_in = pltpu.make_async_copy(bot_hbm, bot, few_sem.at[0])
+    surf_in = pltpu.make_async_copy(surf_hbm, surf, few_sem.at[1])
+    mer_in = pltpu.make_async_copy(mer_hbm, mer, few_sem.at[2])
+    for copy in in_copies(0):
+        copy.start()
+    bot_in.start()
+    surf_in.start()
+    for g in range(1, len(chunks)):
+        for copy in in_copies(g):
+            copy.start()
+    mer_in.start()
+
     barrier = pltpu.get_barrier_semaphore()
 
     def greet(i):
@@ -72,13 +92,11 @@
 
     peers_loop(n, greet)
 
-    for c in range(2):
-        d = bot[col(c), :].astype(jnp.float32)
-        stat[REACH, 4 + c] = d
-        for v in range(2):
-            stat[REACH, 2 * v + c] = jnp.where(d > 0, surf[v, col(c), :], 0.0)
-
-    def gather_chunk(k0, k1):
+    def gather_chunk(g):
+        for copy in in_copies(g):
+            copy.wait()
+        k0, k1 = chunks[g]
+
         def step(k, carry):
             for c in range(2):
                 s_a[c, k, 0] = trc[0, k, col(c), :]
@@ -87,6 +105,16 @@
             return carry
 
         lax.fori_loop(k0, k1, step, 0, unroll=UNROLL)
+
+    gather_chunk(0)
+
+    bot_in.wait()
+    surf_in.wait()
+    for c in range(2):
+        d = bot[col(c), :].astype(jnp.float32)
+        stat[REACH, 4 + c] = d
+        for v in range(2):
+            stat[REACH, 2 * v + c] = jnp.where(d > 0, surf[v, col(c), :], 0.0)
 
     def a_copy(g, side):
         k0, k1 = chunks[g]
@@ -123,14 +151,13 @@
             device_id_type=MESH,
         )
 
-    gather_chunk(*chunks[0])
     pl.semaphore_wait(barrier, n - 1)
+    for side in range(2):
+        a_copy(0, side).start()
     for s in shifts:
         halo_copy(stat, st_send, st_recv, s).start()
-    for side in range(2):
-        a_copy(0, side).start()
     for g in range(1, len(chunks)):
-        gather_chunk(*chunks[g])
+        gather_chunk(g)
         for side in range(2):
             a_copy(g, side).start()
 
@@ -156,6 +183,7 @@
     half = TIME_STEP * 0.25
     diff = TIME_STEP * DIFFUSIVITY
 
+    mer_in.wait()
     for g, (k0, k1) in enumerate(chunks):
         for side in range(2):
             a_copy(g, side).wait_recv()
@@ -387,6 +415,41 @@
         ).wait()
 
 
+def finish(trc, surf, scales, out, sout, gout, buf, sbuf, gbuf, sem):
+    levels = trc.shape[1]
+    chunks = chunk_bounds(levels)
+    scale_one = scales[0:1, 0:1]
+    cross = scales[0:1, 1:2]
+    scale_two = scales[0:1, 2:3]
+    inv_one, inv_two = 1.0 / scale_one, 1.0 / scale_two
+
+    def pair(first, second):
+        unit = first * inv_one
+        return unit, (second - cross * unit) * inv_two
+
+    sbuf[0], sbuf[1] = pair(surf[0], surf[1])
+    gbuf[...] = scales[0:1, 0:3]
+    copies = [
+        pltpu.make_async_copy(sbuf, sout, sem.at[0]),
+        pltpu.make_async_copy(gbuf, gout, sem.at[1]),
+    ]
+    for copy in copies:
+        copy.start()
+    for g, (k0, k1) in enumerate(chunks):
+
+        def step(k, carry):
+            buf[0, k], buf[1, k] = pair(trc[0, k], trc[1, k])
+            return carry
+
+        lax.fori_loop(k0, k1, step, 0, unroll=UNROLL)
+        ks = pl.ds(k0, k1 - k0)
+        copy = pltpu.make_async_copy(buf.at[:, ks], out.at[:, ks], sem.at[2 + g])
+        copy.start()
+        copies.append(copy)
+    for copy in copies:
+        copy.wait()
+
+
 def packed(x):
     lead, (cols, rows) = x.shape[:-2], x.shape[-2:]
     x = x.reshape(lead + (cols, rows // 128, 128))
@@ -415,9 +478,16 @@
             jax.ShapeDtypeStruct((vectors, 16, 128), f32),
             jax.ShapeDtypeStruct((8, 128), f32),
         ),
-        in_specs=[vmem] * 5,
+        in_specs=[pl.BlockSpec(memory_space=pltpu.HBM)] * 5,
         out_specs=(vmem,) * 3,
         scratch_shapes=[
+            pltpu.VMEM((vectors, levels, 16, 128), f32),
+            pltpu.VMEM((vectors, 16, 128), f32),
+            pltpu.VMEM((levels, 16, 128), f32),
+            pltpu.VMEM((levels, 16, 128), f32),
+            pltpu.VMEM((16, 128), jnp.int32),
+            dma((count, 2)),
+            dma((3,)),
             pltpu.VMEM((2, levels, 3, 8, 128), f32),
             pltpu.VMEM((2, levels, 3, 8, 128), f32),
             pltpu.VMEM((2, levels, 2, 8, 128), f32),
@@ -439,7 +509,7 @@
             dma((2,)),
         ],
         compiler_params=pltpu.CompilerParams(
-            collective_id=0, has_side_effects=True, vmem_limit_bytes=40 * 1024 * 1024
+            collective_id=0, has_side_effects=True, vmem_limit_bytes=67043328
         ),
     )(
         packed(tracer_pert),
@@ -448,15 +518,25 @@
         packed(merid_flow),
         packed(bottom_level),
     )
-    growth = tail[0, :3]
-    scale_one, cross, scale_two = growth[0], growth[1], growth[2]
-
-    def renormalized(x):
-        unit = x[0] / scale_one
-        rest = (x[1] - cross * unit) / scale_two
-        return unpacked(jnp.stack([unit, rest]), columns)
-
-    return renormalized(tracer), renormalized(surface), growth
+    hbm = pl.BlockSpec(memory_space=pltpu.HBM)
+    tracer_vec, surface_vec, growth = pl.pallas_call(
+        finish,
+        out_shape=(
+            jax.ShapeDtypeStruct((vectors, levels, 16, 128), f32),
+            jax.ShapeDtypeStruct((vectors, 16, 128), f32),
+            jax.ShapeDtypeStruct((1, 3), f32),
+        ),
+        in_specs=[vmem] * 3,
+        out_specs=(hbm,) * 3,
+        scratch_shapes=[
+            pltpu.VMEM((vectors, levels, 16, 128), f32),
+            pltpu.VMEM((vectors, 16, 128), f32),
+            pltpu.VMEM((1, 3), f32),
+            dma((2 + count,)),
+        ],
+        compiler_params=pltpu.CompilerParams(vmem_limit_bytes=8 * 1024 * 1024),
+    )(tracer, surface, tail)
+    return unpacked(tracer_vec, columns), unpacked(surface_vec, columns), growth.reshape(3)
 
 
 def solution(mesh):

time: 58.8 us -> 52.8 us (0.90)
  other arithmetic: 5.95 us -> 0 us
  Pallas kernels: 46.1 us -> 49.3 us
  local copies, waits for them, and re-layouts: 5.72 us -> 2.53 us
    div x2 -> x0, other arithmetic: 4.03 us -> none  [renormalized(): rest = (x[1] - cross * unit) / scale_two]
    pallas_call x1, Pallas kernels: 46.1 us -> 48.2 us  [on_device(): pl.pallas_call(functools.partial(kernel, n), out_shape=(jax.ShapeDtypeStr...]
    unnamed x10 -> x6, local copies, waits for them, and re-layouts: 4.55 us -> 2.53 us
    reshape x2 -> x0, other arithmetic: 1.93 us -> none  [unpacked(): return x.reshape(lead + (cols, rows // cols * lanes))]
    pallas_call x0 -> x1, Pallas kernels: none -> 1.09 us  [on_device(): pl.pallas_call(finish, out_shape=(jax.ShapeDtypeStruct((vectors, levels,...]
    slice x1 -> x0, local copies, waits for them, and re-layouts: 0.65 us -> none  [on_device(): scale_one, cross, scale_two = (growth[0], growth[1], growth[2])]
where the time goes in v2:
time: 52.8 us; the launch traced here: 52.5 us
  Pallas kernels  49.3 us (93%)
  local copies, waits for them, and re-layouts  2.53 us (5%)
  between operations  0.65 us (1%)
    pallas_call x1, Pallas kernels, on_device(): pl.pallas_call(functools.partial(kernel, n), out_shape=(jax.ShapeDtypeStr...  48.2 us
    unnamed x6, local copies, waits for them, and re-layouts  2.53 us
    pallas_call x1, Pallas kernels, on_device(): pl.pallas_call(finish, out_shape=(jax.ShapeDtypeStruct((vectors, levels,...  1.09 us

profile of v2, /device:TPU:0, one launch (start us, length us, event | category | flops | bytes accessed | tf_op | source)
XLA Modules:
  0.0 52.5 jit_solution(3208087082947600632)
XLA Ops:
  0.6 48.2 %shard_map.76 = (f32[2,50,16,128]{3,2,1,0:T(8,128)}, f32[2,16,128]{2,1,0:T(8,128)}, f32[8,128]{1,0:T(8,128)}) custom-call(f32[2,50,16,128]{3,2,1,0:T(8,128)} %bitcast.36, f32[2,16,128]{2,1,0:T(8,128)} %bitcast.39, f32[50,16,128]{2,1,0:T(8,128)} %bitcast.37, f32[50,16,128]{2,1,0:T(8,128)} %bitcast.38, s32[16,128]{1,0:T(8,128)} %bitcast.40), custom_call_target="tpu_custom_call" | custom-call | tf_op jit(solution)/shard_map/pallas_call | solution.py:474
  48.9 0.0 copy-start.2
  48.9 0.7 %copy-done.2 = f32[8,128]{1,0:T(8,128)S(1)} copy-done((f32[8,128]{1,0:T(8,128)S(1)}, f32[8,128]{1,0:T(8,128)}, u32[]{:S(2)}) %copy-start.2) | copy-done | bytes 4120
  49.6 0.0 copy-start
  49.6 1.1 %copy-done = f32[2,50,16,128]{3,2,1,0:T(8,128)S(1)} copy-done((f32[2,50,16,128]{3,2,1,0:T(8,128)S(1)}, f32[2,50,16,128]{3,2,1,0:T(8,128)}, u32[]{:S(2)}) %copy-start) | copy-done | bytes 819224
  50.7 0.0 copy-start.1
  50.7 0.7 %copy-done.1 = f32[2,16,128]{2,1,0:T(8,128)S(1)} copy-done((f32[2,16,128]{2,1,0:T(8,128)S(1)}, f32[2,16,128]{2,1,0:T(8,128)}, u32[]{:S(2)}) %copy-start.1) | copy-done | bytes 16408
  51.4 1.1 %shard_map.77 = (f32[2,50,16,128]{3,2,1,0:T(8,128)}, f32[2,16,128]{2,1,0:T(8,128)}, f32[1,3]{1,0:T(1,128)}) custom-call(f32[2,50,16,128]{3,2,1,0:T(8,128)S(1)} %copy-done, f32[2,16,128]{2,1,0:T(8,128)S(1)} %copy-done.1, f32[8,128]{1,0:T(8,128)S(1)} %copy-done.2), custom_call_target="tpu_custom_call" | custom-call | tf_op jit(solution)/shard_map/pallas_call | solution.py:522
Async XLA Ops:
  48.9 0.7 %copy-start.2 = (f32[8,128]{1,0:T(8,128)S(1)}, f32[8,128]{1,0:T(8,128)}, u32[]{:S(2)}) copy-start(f32[8,128]{1,0:T(8,128)} %get-tuple-element.11.scales) | copy-start | bytes 12292
  49.6 1.1 %copy-start = (f32[2,50,16,128]{3,2,1,0:T(8,128)S(1)}, f32[2,50,16,128]{3,2,1,0:T(8,128)}, u32[]{:S(2)}) copy-start(f32[2,50,16,128]{3,2,1,0:T(8,128)} %get-tuple-element.9.trc) | copy-start | bytes 2457604
  50.7 0.7 %copy-start.1 = (f32[2,16,128]{2,1,0:T(8,128)S(1)}, f32[2,16,128]{2,1,0:T(8,128)}, u32[]{:S(2)}) copy-start(f32[2,16,128]{2,1,0:T(8,128)} %get-tuple-element.10.surf) | copy-start | bytes 49156

commit v3 on v2

--- a/solution.py
+++ b/solution.py
@@ -13,8 +13,8 @@
 STERIC_GAIN = 2.0
 EPSILON = 1e-06
 MESH = pl.DeviceIdType.MESH
-CHUNKS = 5
-UNROLL = 2
+CHUNKS = 4
+UNROLL = 5
 REACH = 2
 
 
@@ -38,8 +38,8 @@
 
 
 def kernel(
-    n, trc_hbm, surf_hbm, zon_hbm, mer_hbm, bot_hbm, out, sout, gout,
-    trc, surf, zon, mer, bot, in_sem, few_sem, s_a, r_a, s_b, r_b, coef, stat, ster, pack, red,
+    n, trc_hbm, surf_hbm, zon_hbm, mer_hbm, bot_hbm, out_hbm, sout, gout,
+    out, out_sem, trc, surf, zon, mer, bot, in_sem, few_sem, s_a, r_a, s_b, r_b, coef, stat, ster, pack, red,
     a_send, a_recv, b_send, b_recv, st_send, st_recv, se_send, se_recv, rd_send, rd_recv,
 ):
     me = lax.axis_index("lon")
@@ -70,6 +70,11 @@
             pltpu.make_async_copy(trc_hbm.at[:, ks], trc.at[:, ks], in_sem.at[g, 0]),
             pltpu.make_async_copy(zon_hbm.at[ks], zon.at[ks], in_sem.at[g, 1]),
         )
+
+    def out_copy(g):
+        k0, k1 = chunks[g]
+        ks = pl.ds(k0, k1 - k0)
+        return pltpu.make_async_copy(out.at[:, ks], out_hbm.at[:, ks], out_sem.at[g])
 
     bot_in = pltpu.make_async_copy(bot_hbm, bot, few_sem.at[0])
     surf_in = pltpu.make_async_copy(surf_hbm, surf, few_sem.at[1])
@@ -266,6 +271,7 @@
             return tuple(sums + grams)
 
         totals = lax.fori_loop(k0, k1, second, totals, unroll=UNROLL)
+        out_copy(g).start()
 
     for q in range(4):
         ster[REACH, q] = totals[q]
@@ -403,6 +409,7 @@
     gout[...] = growth
 
     for g in range(len(chunks)):
+        out_copy(g).wait()
         for side in range(2):
             a_copy(g, side).wait_send()
             b_copy(g, side).wait_send()
@@ -415,9 +422,23 @@
         ).wait()
 
 
-def finish(trc, surf, scales, out, sout, gout, buf, sbuf, gbuf, sem):
+def finish(
+    trc_hbm, surf_hbm, scales_hbm, out, sout, gout,
+    trc, surf, scales, in_sem, buf, sbuf, gbuf, sem,
+):
     levels = trc.shape[1]
     chunks = chunk_bounds(levels)
+    scales_in = pltpu.make_async_copy(scales_hbm, scales, in_sem.at[0])
+    surf_in = pltpu.make_async_copy(surf_hbm, surf, in_sem.at[1])
+    scales_in.start()
+    surf_in.start()
+    ins = []
+    for g, (k0, k1) in enumerate(chunks):
+        ks = pl.ds(k0, k1 - k0)
+        ins.append(pltpu.make_async_copy(trc_hbm.at[:, ks], trc.at[:, ks], in_sem.at[2 + g]))
+        ins[-1].start()
+    scales_in.wait()
+    surf_in.wait()
     scale_one = scales[0:1, 0:1]
     cross = scales[0:1, 1:2]
     scale_two = scales[0:1, 2:3]
@@ -441,6 +462,7 @@
             buf[0, k], buf[1, k] = pair(trc[0, k], trc[1, k])
             return carry
 
+        ins[g].wait()
         lax.fori_loop(k0, k1, step, 0, unroll=UNROLL)
         ks = pl.ds(k0, k1 - k0)
         copy = pltpu.make_async_copy(buf.at[:, ks], out.at[:, ks], sem.at[2 + g])
@@ -479,8 +501,10 @@
             jax.ShapeDtypeStruct((8, 128), f32),
         ),
         in_specs=[pl.BlockSpec(memory_space=pltpu.HBM)] * 5,
-        out_specs=(vmem,) * 3,
+        out_specs=(pl.BlockSpec(memory_space=pltpu.HBM), vmem, vmem),
         scratch_shapes=[
+            pltpu.VMEM((vectors, levels, 16, 128), f32),
+            dma((count,)),
             pltpu.VMEM((vectors, levels, 16, 128), f32),
             pltpu.VMEM((vectors, 16, 128), f32),
             pltpu.VMEM((levels, 16, 128), f32),
@@ -526,15 +550,19 @@
             jax.ShapeDtypeStruct((vectors, 16, 128), f32),
             jax.ShapeDtypeStruct((1, 3), f32),
         ),
-        in_specs=[vmem] * 3,
+        in_specs=[hbm] * 3,
         out_specs=(hbm,) * 3,
         scratch_shapes=[
+            pltpu.VMEM((vectors, levels, 16, 128), f32),
+            pltpu.VMEM((vectors, 16, 128), f32),
+            pltpu.VMEM((8, 128), f32),
+            dma((2 + count,)),
             pltpu.VMEM((vectors, levels, 16, 128), f32),
             pltpu.VMEM((vectors, 16, 128), f32),
             pltpu.VMEM((1, 3), f32),
             dma((2 + count,)),
         ],
-        compiler_params=pltpu.CompilerParams(vmem_limit_bytes=8 * 1024 * 1024),
+        compiler_params=pltpu.CompilerParams(vmem_limit_bytes=67043328),
     )(tracer, surface, tail)
     return unpacked(tracer_vec, columns), unpacked(surface_vec, columns), growth.reshape(3)
 

time: 52.8 us -> 51.1 us (0.968)
  local copies, waits for them, and re-layouts: 2.53 us -> 0 us
  Pallas kernels: 49.3 us -> 50.3 us
    unnamed x6 -> x0, local copies, waits for them, and re-layouts: 2.53 us -> none
    pallas_call x1, Pallas kernels: 1.09 us -> 2.08 us  [on_device(): pl.pallas_call(finish, out_shape=(jax.ShapeDtypeStruct((vectors, levels,...]
where the time goes in v3:
time: 51.1 us; the launch traced here: 50.9 us
  Pallas kernels  50.3 us (98%)
  between operations  0.64 us (1%)
    pallas_call x1, Pallas kernels, on_device(): pl.pallas_call(functools.partial(kernel, n), out_shape=(jax.ShapeDtypeStr...  48.2 us
    pallas_call x1, Pallas kernels, on_device(): pl.pallas_call(finish, out_shape=(jax.ShapeDtypeStruct((vectors, levels,...  2.08 us

profile of v3, /device:TPU:0, one launch (start us, length us, event | category | flops | bytes accessed | tf_op | source)
XLA Modules:
  0.0 50.9 jit_solution(8658005253212694495)
XLA Ops:
  0.6 48.2 %shard_map.76 = (f32[2,50,16,128]{3,2,1,0:T(8,128)}, f32[2,16,128]{2,1,0:T(8,128)}, f32[8,128]{1,0:T(8,128)}) custom-call(f32[2,50,16,128]{3,2,1,0:T(8,128)} %bitcast.36, f32[2,16,128]{2,1,0:T(8,128)} %bitcast.39, f32[50,16,128]{2,1,0:T(8,128)} %bitcast.37, f32[50,16,128]{2,1,0:T(8,128)} %bitcast.38, s32[16,128]{1,0:T(8,128)} %bitcast.40), custom_call_target="tpu_custom_call" | custom-call | tf_op jit(solution)/shard_map/pallas_call | solution.py:496
  48.9 2.1 %shard_map.77 = (f32[2,50,16,128]{3,2,1,0:T(8,128)}, f32[2,16,128]{2,1,0:T(8,128)}, f32[1,3]{1,0:T(1,128)}) custom-call(f32[2,50,16,128]{3,2,1,0:T(8,128)} %get-tuple-element.9.trc_hbm, f32[2,16,128]{2,1,0:T(8,128)} %get-tuple-element.10.surf_hbm, f32[8,128]{1,0:T(8,128)} %get-tuple-element.11.scales_hbm), custom_call_target="tpu_custom_call" | custom-call | tf_op jit(solution)/shard_map/pallas_call | solution.py:546

commit v4 on v3

--- a/solution.py
+++ b/solution.py
@@ -13,14 +13,13 @@
 STERIC_GAIN = 2.0
 EPSILON = 1e-06
 MESH = pl.DeviceIdType.MESH
-CHUNKS = 4
+CHUNK_EDGES = (0, 34, 64, 88, 100)
 UNROLL = 5
 REACH = 2
 
 
 def chunk_bounds(levels):
-    count = min(CHUNKS, levels)
-    edges = [levels * i // count for i in range(count + 1)]
+    edges = sorted({levels * part // 100 for part in CHUNK_EDGES})
     return list(zip(edges[:-1], edges[1:]))
 
 
@@ -166,7 +165,7 @@
         for side in range(2):
             a_copy(g, side).start()
 
-    for s in shifts:
+    for s in shifts[:2]:
         halo_copy(stat, st_send, st_recv, s).wait_recv()
     width = 2 * (2 * REACH + 1)
     mid = 2 * REACH
@@ -230,6 +229,9 @@
         for side in range(2):
             b_copy(g, side).start()
 
+    for s in shifts[2:]:
+        halo_copy(stat, st_send, st_recv, s).wait_recv()
+
     face_x = {i: SURFACE_COUPLING * x_face(i) for i in range(0, width - 1)}
     face_y = {i: SURFACE_COUPLING * y_face(i) for i in range(1, width - 1)}
 
@@ -295,8 +297,8 @@
         mine = zero
         for q, part in enumerate(parts):
             mine = jnp.where(lane == q, total_of(part), mine)
-        pack[turn] = mine
-        red[turn, me] = mine
+        pack[turn] = mine[0:1]
+        red[turn, me] = mine[0:1]
         peers_loop(n, lambda i: red_copy(turn, i).start())
         every = pltpu.make_async_copy(
             red.at[turn, pl.ds(0, n - 1)], red.at[turn, pl.ds(0, n - 1)], rd_recv.at[turn]
@@ -519,8 +521,8 @@
             pltpu.VMEM((levels, 10, 8, 128), f32),
             pltpu.VMEM((slots, 6, 8, 128), f32),
             pltpu.VMEM((slots, 4, 8, 128), f32),
-            pltpu.VMEM((2, 8, 128), f32),
-            pltpu.VMEM((2, n, 8, 128), f32),
+            pltpu.VMEM((2, 1, 128), f32),
+            pltpu.VMEM((2, n, 1, 128), f32),
             dma((2, count)),
             dma((2, count)),
             dma((2, count)),

time: 51.1 us -> 48.9 us (0.957)
  Pallas kernels: 50.3 us -> 48.1 us
    pallas_call x1, Pallas kernels: 48.2 us -> 46.1 us  [on_device(): pl.pallas_call(functools.partial(kernel, n), out_shape=(jax.ShapeDtypeStr...]
where the time goes in v4:
time: 48.9 us; the launch traced here: 48.8 us
  Pallas kernels  48.1 us (98%)
  between operations  0.64 us (1%)
    pallas_call x1, Pallas kernels, on_device(): pl.pallas_call(functools.partial(kernel, n), out_shape=(jax.ShapeDtypeStr...  46.1 us
    pallas_call x1, Pallas kernels, on_device(): pl.pallas_call(finish, out_shape=(jax.ShapeDtypeStruct((vectors, levels,...  2 us

profile of v4, /device:TPU:0, one launch (start us, length us, event | category | flops | bytes accessed | tf_op | source)
XLA Modules:
  0.0 48.8 jit_solution(3888881163215141984)
XLA Ops:
  0.6 46.1 %shard_map.76 = (f32[2,50,16,128]{3,2,1,0:T(8,128)}, f32[2,16,128]{2,1,0:T(8,128)}, f32[8,128]{1,0:T(8,128)}) custom-call(f32[2,50,16,128]{3,2,1,0:T(8,128)} %bitcast.36, f32[2,16,128]{2,1,0:T(8,128)} %bitcast.39, f32[50,16,128]{2,1,0:T(8,128)} %bitcast.37, f32[50,16,128]{2,1,0:T(8,128)} %bitcast.38, s32[16,128]{1,0:T(8,128)} %bitcast.40), custom_call_target="tpu_custom_call" | custom-call | tf_op jit(solution)/shard_map/pallas_call | solution.py:498
  46.8 2.0 %shard_map.77 = (f32[2,50,16,128]{3,2,1,0:T(8,128)}, f32[2,16,128]{2,1,0:T(8,128)}, f32[1,3]{1,0:T(1,128)}) custom-call(f32[2,50,16,128]{3,2,1,0:T(8,128)} %get-tuple-element.9.trc_hbm, f32[2,16,128]{2,1,0:T(8,128)} %get-tuple-element.10.surf_hbm, f32[8,128]{1,0:T(8,128)} %get-tuple-element.11.scales_hbm), custom_call_target="tpu_custom_call" | custom-call | tf_op jit(solution)/shard_map/pallas_call | solution.py:548

commit v5 on v4

--- a/solution.py
+++ b/solution.py
@@ -62,6 +62,15 @@
     def col(c):
         return pl.ds(c, 8, stride=2)
 
+    barrier = pltpu.get_barrier_semaphore()
+
+    def greet(i):
+        pl.semaphore_signal(
+            barrier, inc=1, device_id={"lon": lax.rem(me + i, n)}, device_id_type=MESH
+        )
+
+    peers_loop(n, greet)
+
     def in_copies(g):
         k0, k1 = chunks[g]
         ks = pl.ds(k0, k1 - k0)
@@ -78,23 +87,14 @@
     bot_in = pltpu.make_async_copy(bot_hbm, bot, few_sem.at[0])
     surf_in = pltpu.make_async_copy(surf_hbm, surf, few_sem.at[1])
     mer_in = pltpu.make_async_copy(mer_hbm, mer, few_sem.at[2])
+    bot_in.start()
+    surf_in.start()
     for copy in in_copies(0):
         copy.start()
-    bot_in.start()
-    surf_in.start()
     for g in range(1, len(chunks)):
         for copy in in_copies(g):
             copy.start()
     mer_in.start()
-
-    barrier = pltpu.get_barrier_semaphore()
-
-    def greet(i):
-        pl.semaphore_signal(
-            barrier, inc=1, device_id={"lon": lax.rem(me + i, n)}, device_id_type=MESH
-        )
-
-    peers_loop(n, greet)
 
     def gather_chunk(g):
         for copy in in_copies(g):
@@ -109,8 +109,6 @@
             return carry
 
         lax.fori_loop(k0, k1, step, 0, unroll=UNROLL)
-
-    gather_chunk(0)
 
     bot_in.wait()
     surf_in.wait()
@@ -155,6 +153,7 @@
             device_id_type=MESH,
         )
 
+    gather_chunk(0)
     pl.semaphore_wait(barrier, n - 1)
     for side in range(2):
         a_copy(0, side).start()
@@ -277,7 +276,7 @@
 
     for q in range(4):
         ster[REACH, q] = totals[q]
-    for s in shifts:
+    for s in reversed(shifts):
         halo_copy(ster, se_send, se_recv, s).start()
 
     def total_of(x):

time: 48.9 us -> 48.8 us (level)
  no operation moved by 1% of the time
where the time goes in v5:
time: 48.8 us; the launch traced here: 48.6 us
  Pallas kernels  47.9 us (98%)
  between operations  0.64 us (1%)
    pallas_call x1, Pallas kernels, on_device(): pl.pallas_call(functools.partial(kernel, n), out_shape=(jax.ShapeDtypeStr...  45.9 us
    pallas_call x1, Pallas kernels, on_device(): pl.pallas_call(finish, out_shape=(jax.ShapeDtypeStruct((vectors, levels,...  2 us

profile of v5, /device:TPU:0, one launch (start us, length us, event | category | flops | bytes accessed | tf_op | source)
XLA Modules:
  0.0 48.6 jit_solution(330205498759325565)
XLA Ops:
  0.6 45.9 %shard_map.76 = (f32[2,50,16,128]{3,2,1,0:T(8,128)}, f32[2,16,128]{2,1,0:T(8,128)}, f32[8,128]{1,0:T(8,128)}) custom-call(f32[2,50,16,128]{3,2,1,0:T(8,128)} %bitcast.36, f32[2,16,128]{2,1,0:T(8,128)} %bitcast.39, f32[50,16,128]{2,1,0:T(8,128)} %bitcast.37, f32[50,16,128]{2,1,0:T(8,128)} %bitcast.38, s32[16,128]{1,0:T(8,128)} %bitcast.40), custom_call_target="tpu_custom_call" | custom-call | tf_op jit(solution)/shard_map/pallas_call | solution.py:497
  46.6 2.0 %shard_map.77 = (f32[2,50,16,128]{3,2,1,0:T(8,128)}, f32[2,16,128]{2,1,0:T(8,128)}, f32[1,3]{1,0:T(1,128)}) custom-call(f32[2,50,16,128]{3,2,1,0:T(8,128)} %get-tuple-element.9.trc_hbm, f32[2,16,128]{2,1,0:T(8,128)} %get-tuple-element.10.surf_hbm, f32[8,128]{1,0:T(8,128)} %get-tuple-element.11.scales_hbm), custom_call_target="tpu_custom_call" | custom-call | tf_op jit(solution)/shard_map/pallas_call | solution.py:547
